TPU v7x, 256 devices: a whole 4x4x8 slice. The times are simulated.
256 devices in a mesh: samp: 8 (over y, core), par: 32 (over z, x).
Axes of the slice: x: 4, y: 4, z: 8, core: 2. Of those that a mesh axis runs over, the one named last changes fastest.
Arguments:
- jacobian: bfloat16 [8192, 65536], P(('samp', 'par')), as said below
- sample_slot: int32 [8192], P(('samp', 'par')), may hold values from 0 to 1023, as said below
- panel_index: int32 [1], replicated, may hold values from 0 to 8191
- shift_value: float32 [1], replicated, may hold values from 0.1 to 1
Outputs:
- cholesky_panel: float32 [8192, 1024], P(('samp', 'par'))
Inputs may be any that keep to these rules, and one draw needn't show every extreme that they name: Within each group (samples g * 1024 to (g + 1) * 1024 - 1), sample_slot is a permutation of 0 to 1023. `jacobian`: finite values.
All inputs are finite; a program needn't handle non-finite values.
Results may differ from a plain program's by a relative error of at most 0.0003.
Values may be sent and summed in bfloat16 or wider, within the bound.
A program may use at most 128 MiB of HBM per device.

v0:
```python
import jax
import jax.numpy as jnp
from jax import lax
from jax.sharding import Mesh
from jax.sharding import PartitionSpec as P

PAR = ("par_0", "par_1")
SAMP_PAR = ("samp", "par_0", "par_1")


def sent_to_all(shard, axis):
    peers = lax.axis_size(axis)
    return lax.all_to_all(
        jnp.broadcast_to(shard[None], (peers, *shard.shape)), axis, 0, 0, tiled=True
    )


def laid_out(tiles, dim):
    tiles = jnp.moveaxis(tiles, 0, dim)
    dims = tiles.shape
    return tiles.reshape(*dims[:dim], dims[dim] * dims[dim + 1], *dims[dim + 2 :])


def gather_directly(shard, axis, dim):
    tiles = sent_to_all(shard, axis)
    return laid_out(tiles, dim)


def padded_to(lines, peers):
    spare = -len(lines) % peers
    return jnp.pad(lines, [(0, spare)] + [(0, 0)] * (lines.ndim - 1))


def spread(shard, axis, root):
    lines = jnp.where(lax.axis_index(axis) == root, shard, jnp.zeros_like(shard)).reshape(
        -1, *shard.shape[1:][-1:]
    )
    padded = padded_to(lines, lax.axis_size(axis))
    own = lax.psum_scatter(padded, axis, scatter_dimension=0, tiled=True)
    return lax.all_gather(own, axis, axis=0, tiled=True)[: len(lines)].reshape(shard.shape)


def sum_by_axis(shard, axes, dim):
    if not axes:
        return shard
    nearer = lax.psum_scatter(shard, axes[0], scatter_dimension=dim, tiled=True)
    return sum_by_axis(nearer, axes[1:], dim)


def invert_factor(block, identity_matrix):
    factor = jnp.linalg.cholesky(block)
    return lax.linalg.triangular_solve(factor, identity_matrix, left_side=True, lower=True)


def on_device(jacobian, sample_slot, panel_index, shift_value):
    arrived = lax.all_to_all(jacobian, PAR, split_axis=1, concat_axis=0, tiled=True)
    own_slots = gather_directly(sample_slot, PAR, 0)
    inverse = jnp.argsort(own_slots)
    ordered = jnp.take(arrived, inverse, axis=0)
    group_width = ordered.shape[0]
    pivot_group = panel_index[0] // group_width
    rotation = panel_index[0] % group_width
    pivot_rows = jnp.roll(spread(ordered, "samp", pivot_group), -rotation, axis=0)
    partial_gram = lax.dot_general(
        ordered, pivot_rows, (((1,), (1,)), ((), ())), preferred_element_type=jnp.float32
    )
    share = group_width // lax.axis_size(PAR)
    samples = group_width * lax.axis_size("samp")
    identity_matrix = jnp.eye(group_width, dtype=jnp.float32)
    shifted_eye = jnp.roll(identity_matrix, -rotation, axis=1)
    on_pivot = (lax.axis_index("samp") == pivot_group).astype(jnp.float32)
    shift_term = shift_value[0] * on_pivot
    start = lax.axis_index(PAR) * share
    summed = sum_by_axis(partial_gram, PAR, 0)
    band = lax.dynamic_slice_in_dim(shifted_eye, start, share, 0)
    my_rows = summed / samples + shift_term * band
    pivot_partial = lax.dot_general(
        pivot_rows, pivot_rows, (((1,), (1,)), ((), ())), preferred_element_type=jnp.float32
    )
    pivot_sum = lax.psum(pivot_partial, PAR)
    pivot_block = pivot_sum / samples + shift_value[0] * identity_matrix
    inverse_factor = invert_factor(pivot_block, identity_matrix)
    return lax.dot_general(
        my_rows,
        inverse_factor,
        (((1,), (1,)), ((), ())),
        precision=lax.Precision.HIGHEST,
        preferred_element_type=jnp.float32,
    )


def solution(mesh):
    torus = Mesh(mesh.devices.reshape(mesh.shape["samp"], 8, 4), ("samp", "par_0", "par_1"))
    return jax.shard_map(
        on_device,
        mesh=torus,
        in_specs=(P(SAMP_PAR, None), P(SAMP_PAR), P(), P()),
        out_specs=P(SAMP_PAR, None),
        check_vma=False,
    )
```

profile of v0, /device:TPU:8, one launch (start us, length us, event | category | flops | bytes accessed | tf_op | source)
XLA Modules:
  0.0 796.8 jit_solution(5502740099929445992)
XLA Ops:
  7.8 11.3 %all-to-all-start = ((s32[32,1,32]{2,1,0:T(1,128)}), s32[32,1,32]{2,1,0:T(1,128)S(1)}, u32[]{:S(2)}, u32[]{:S(2)}) async-start(s32[32,1,32]{2,1,0:T(1,128)} %broadcast_in_dim.23), calls=%async_computation | async-start | bytes 32768 | tf_op jit(solution)/shard_map/all_to_all | solution.py:13
  40.2 87.4 %all-to-all-done.1 = bf16[32,32,2048]{2,0,1:T(8,128)(2,1)} async-done(((bf16[32,32,2048]{2,0,1:T(8,128)(2,1)}), bf16[32,32,2048]{2,0,1:T(8,128)(2,1)}, u32[]{:S(2)}, u32[]{:S(2)}) %all-to-all-start.1) | async-done | bytes 4194336 | tf_op jit(solution)/shard_map/all_to_all | solution.py:56
  127.6 11.6 %gather_fusion = bf16[1024,2048]{1,0:T(8,128)(2,1)} fusion(bf16[1024,2048]{1,0:T(8,128)(2,1)} %bitcast.1, s32[1024]{0:T(1024)S(1)} %fusion.77), kind=kCustom, calls=%fused_computation | custom fusion | bytes 8392704 | tf_op jit(solution)/shard_map/jit(_take)/gather | solution.py:59
  143.2 35.1 %reduce-scatter.6.cloned.1.call-done = bf16[128,2048]{1,0:T(8,128)(2,1)} async-done(((bf16[1024,2048]{1,0:T(8,128)(2,1)}), bf16[128,2048]{1,0:T(8,128)(2,1)}) %reduce-scatter.6.cloned.1.call-update) | async-done | bytes 524304 | tf_op jit(solution)/shard_map/reduce_scatter | solution.py:39
  178.4 37.8 %all-gather.2.cloned.1.call-done = bf16[1024,2048]{1,0:T(8,128)(2,1)} async-done(((bf16[128,2048]{1,0:T(8,128)(2,1)}), bf16[1024,2048]{1,0:T(8,128)(2,1)}) %all-gather.2.cloned.1.call-update) | async-done | bytes 4194320 | tf_op jit(solution)/shard_map/all_gather | solution.py:40
  216.2 13.5 %fusion.85 = f32[1024,1024]{0,1:T(8,128)} fusion(s32[]{:T(128)S(6)} %select_n.64, bf16[1024,2048]{1,0:T(8,128)(2,1)} %all-gather.2.cloned.1.call-done), kind=kOutput, calls=%fused_computation.182 | convolution fusion | flops 4303355904 | bytes 8388612 | tf_op jit(solution)/shard_map/dot_general | solution.py:77
  234.4 9.8 %fusion.11 = f32[1024,1024]{0,1:T(8,128)} fusion(bf16[1024,2048]{1,0:T(8,128)(2,1)S(1)} %copy-done.2, pred[1024]{0:T(1024)(128)(4,1)S(1)} %compare_and_fusion, s32[]{:T(128)S(6)} %select_n.64, bf16[1024,2048]{1,0:T(8,128)(2,1)} %all-gather.2.cloned.1.call-done), kind=kOutput, calls=%fused_computation.26 | convolution fusion | flops 4305453056 | bytes 12583940 | tf_op jit(solution)/shard_map/dot_general | solution.py:64
  244.3 150.8 %all-reduce.3.cloned.1.call-done = f32[1024,1024]{0,1:T(8,128)} async-done(((f32[1024,1024]{0,1:T(8,128)}), f32[1024,1024]{0,1:T(8,128)}) %all-reduce.3.cloned.1.call-update) | async-done | bytes 4194320 | tf_op jit(solution)/shard_map/psum | solution.py:80
  412.2 11.7 %cholesky.222 = f32[128,128]{1,0:T(8,128)S(1)} custom-call(f32[128,128]{1,0:T(8,128)S(1)} %cholesky.577), custom_call_target="Cholesky" | custom-call | tf_op jit(solution)/shard_map/jit(cholesky)/cholesky | solution.py:51
  424.1 9.8 %custom-call.62 = f32[1,128,128]{1,2,0:T(8,128)S(1)} custom-call(f32[1,128,128]{2,1,0:T(8,128)S(1)} %get-tuple-element.71), custom_call_target="InvertDiagBlocksLowerTriangular" | custom-call | tf_op jit(solution)/shard_map/jit(cholesky)/cholesky | solution.py:51
  437.2 11.7 %cholesky.243 = f32[128,128]{1,0:T(8,128)S(1)} custom-call(f32[128,128]{1,0:T(8,128)S(1)} %cholesky.581), custom_call_target="Cholesky" | custom-call | tf_op jit(solution)/shard_map/jit(cholesky)/cholesky | solution.py:51
  449.4 9.8 %custom-call.63 = f32[1,128,128]{1,2,0:T(8,128)S(1)} custom-call(f32[1,128,128]{2,1,0:T(8,128)S(1)} %get-tuple-element.69), custom_call_target="InvertDiagBlocksLowerTriangular" | custom-call | tf_op jit(solution)/shard_map/jit(cholesky)/cholesky | solution.py:51
  464.7 11.7 %cholesky.466 = f32[128,128]{1,0:T(8,128)S(1)} custom-call(f32[128,128]{1,0:T(8,128)S(1)} %cholesky.586), custom_call_target="Cholesky" | custom-call | tf_op jit(solution)/shard_map/jit(cholesky)/cholesky | solution.py:51
  477.2 9.8 %custom-call.64 = f32[1,128,128]{1,2,0:T(8,128)S(1)} custom-call(f32[1,128,128]{2,1,0:T(8,128)S(1)} %get-tuple-element.67), custom_call_target="InvertDiagBlocksLowerTriangular" | custom-call | tf_op jit(solution)/shard_map/jit(cholesky)/cholesky | solution.py:51
  491.6 11.7 %cholesky.485 = f32[128,128]{1,0:T(8,128)S(1)} custom-call(f32[128,128]{1,0:T(8,128)S(1)} %cholesky.591), custom_call_target="Cholesky" | custom-call | tf_op jit(solution)/shard_map/jit(cholesky)/cholesky | solution.py:51
  504.1 9.8 %custom-call.65 = f32[1,128,128]{1,2,0:T(8,128)S(1)} custom-call(f32[1,128,128]{2,1,0:T(8,128)S(1)} %get-tuple-element.65), custom_call_target="InvertDiagBlocksLowerTriangular" | custom-call | tf_op jit(solution)/shard_map/jit(cholesky)/cholesky | solution.py:51
  518.2 12.1 %cholesky.504 = f32[128,128]{1,0:T(8,128)S(1)} custom-call(f32[128,128]{1,0:T(8,128)S(1)} %cholesky.596), custom_call_target="Cholesky" | custom-call | tf_op jit(solution)/shard_map/jit(cholesky)/cholesky | solution.py:51
  531.1 9.8 %custom-call.66 = f32[1,128,128]{1,2,0:T(8,128)S(1)} custom-call(f32[1,128,128]{2,1,0:T(8,128)S(1)} %get-tuple-element.63), custom_call_target="InvertDiagBlocksLowerTriangular" | custom-call | tf_op jit(solution)/shard_map/jit(cholesky)/cholesky | solution.py:51
  545.1 11.7 %cholesky.524 = f32[128,128]{1,0:T(8,128)S(1)} custom-call(f32[128,128]{1,0:T(8,128)S(1)} %cholesky.601), custom_call_target="Cholesky" | custom-call | tf_op jit(solution)/shard_map/jit(cholesky)/cholesky | solution.py:51
  557.6 9.8 %custom-call.67 = f32[1,128,128]{1,2,0:T(8,128)S(1)} custom-call(f32[1,128,128]{2,1,0:T(8,128)S(1)} %get-tuple-element.61), custom_call_target="InvertDiagBlocksLowerTriangular" | custom-call | tf_op jit(solution)/shard_map/jit(cholesky)/cholesky | solution.py:51
  571.3 11.7 %cholesky.544 = f32[128,128]{1,0:T(8,128)S(1)} custom-call(f32[128,128]{1,0:T(8,128)S(1)} %cholesky.606), custom_call_target="Cholesky" | custom-call | tf_op jit(solution)/shard_map/jit(cholesky)/cholesky | solution.py:51
  596.6 11.7 %cholesky.562 = f32[128,128]{1,0:T(8,128)S(1)} custom-call(f32[128,128]{1,0:T(8,128)S(1)} %convolution_subtract_fusion.11), custom_call_target="Cholesky" | custom-call | tf_op jit(solution)/shard_map/jit(cholesky)/cholesky | solution.py:51
  623.5 24.0 %while.1 = (s32[]{:T(128)}, f32[1024,1024]{0,1:T(8,128)}, s32[8,2]{0,1:T(2,128)S(1)}, f32[8,128,128]{2,1,0:T(8,128)S(1)}, s32[]{:T(128)}) while((s32[]{:T(128)}, f32[1024,1024]{0,1:T(8,128)}, s32[8,2]{0,1:T(2,128)S(1)}, f32[8,128,128]{2,1,0:T(8,128)S(1)}, s32[]{:T(128)}) %tuple.51), condition=%wide.while_cond, body=%wide.while_body.sunk | while | flops 2 | bytes 393329 | solution.py:52
  647.5 79.6 %custom-call.69 = f32[8,128,128]{1,2,0:T(8,128)} custom-call(f32[8,128,128]{2,1,0:T(8,128)S(1)} %get-tuple-element.14), custom_call_target="InvertDiagBlocksLowerTriangular" | custom-call | tf_op jit(solution)/shard_map/triangular_solve | solution.py:52
  (156 shorter events, 186.3 us)
Async XLA Ops:
  7.8 21.0 %all-to-all-start = ((s32[32,1,32]{2,1,0:T(1,128)}), s32[32,1,32]{2,1,0:T(1,128)S(1)}, u32[]{:S(2)}, u32[]{:S(2)}) async-start(s32[32,1,32]{2,1,0:T(1,128)} %broadcast_in_dim.23), calls=%async_computation | async-start | bytes 32768 | tf_op jit(solution)/shard_map/all_to_all | solution.py:13
  28.8 98.8 %all-to-all-start.1 = ((bf16[32,32,2048]{2,0,1:T(8,128)(2,1)}), bf16[32,32,2048]{2,0,1:T(8,128)(2,1)}, u32[]{:S(2)}, u32[]{:S(2)}) async-start(bf16[32,32,2048]{2,0,1:T(8,128)(2,1)} %bitcast.117), calls=%async_computation.1 | async-start | bytes 8388608 | tf_op jit(solution)/shard_map/all_to_all | solution.py:56
  33.8 144.5 %reduce-scatter.6.cloned.1.call-start = ((), (), s32[]{:S(2)}) async-start(), calls=%async_computation.5 | async-start | bytes 4718592 | tf_op jit(solution)/shard_map/reduce_scatter | solution.py:39
  143.1 73.1 %all-gather.2.cloned.1.call-start = ((), (), s32[]{:S(2)}) async-start(), calls=%async_computation.6 | async-start | bytes 4718592 | tf_op jit(solution)/shard_map/all_gather | solution.py:40
  178.4 216.8 %all-reduce.3.cloned.1.call-start = ((), (), s32[]{:S(2)}) async-start(), calls=%async_computation.8 | async-start | bytes 8388608 | tf_op jit(solution)/shard_map/psum | solution.py:80
  229.7 528.2 %reduce-scatter.8.cloned.1.call-start = ((), (), s32[]{:S(2)}) async-start(), calls=%async_computation.7 | async-start | bytes 4718592 | tf_op jit(solution)/shard_map/reduce_scatter | solution.py:46
  230.7 3.7 copy-start.2
  244.3 537.1 %reduce-scatter.10.cloned.1.call-start = ((), (), s32[]{:S(2)}) async-start(), calls=%async_computation.9 | async-start | bytes 655360
  410.2 2.0 copy-start.3
  460.3 2.0 copy-start
  727.1 7.4 copy-start.1
  729.7 7.6 copy-start.4
Sparse Core Ops, SparseCore 0:
  143.3 35.0 reduce-scatter.5
  180.2 35.9 all-gather.1
  229.9 165.2 all-reduce.2
  397.5 52.5 reduce-scatter.7
  760.2 21.1 reduce-scatter.9
where the time goes:
time: 806 us; the launch traced here: 797 us
  waiting for transfers between devices  318 us (39%)
  other arithmetic  274 us (34%)
  matrix products  107 us (13%)
  local copies, waits for them, and re-layouts  60.1 us (7%)
  between operations  20.3 us (3%)
  starting transfers between devices  16.7 us (2%)
    another operation x30, other arithmetic, invert_factor(): factor = jnp.linalg.cholesky(block)  167 us
    psum x1, waiting for transfers between devices, on_device(): pivot_sum = lax.psum(pivot_partial, PAR)  151 us
    all_to_all x1, waiting for transfers between devices, on_device(): lax.all_to_all(jacobian, PAR, split_axis=1, concat_axis=0, tiled=True)  87.4 us
    another operation x3, other arithmetic, invert_factor(): lax.linalg.triangular_solve(factor, identity_matrix, left_side=True, lowe...  84.5 us
    another operation x15, matrix products, invert_factor(): lax.linalg.triangular_solve(factor, identity_matrix, left_side=True, lowe...  50.3 us
    all_gather x1, waiting for transfers between devices, spread(): lax.all_gather(own, axis, axis=0, tiled=True)[:len(lines)]  37.8 us
    reduce_scatter x1, waiting for transfers between devices, spread(): own = lax.psum_scatter(padded, axis, scatter_dimension=0, tiled=True)  35.1 us
    another operation x14, matrix products, invert_factor(): factor = jnp.linalg.cholesky(block)  25.9 us
  transfers between devices with their start and end apart: 7, of which 6 were waited for; matrix products, arithmetic and copies ran while one was open for 50% of the time, Pallas kernels for 0%

commit v1 on v0

--- a/solution.py
+++ b/solution.py
@@ -77,7 +77,9 @@
     pivot_partial = lax.dot_general(
         pivot_rows, pivot_rows, (((1,), (1,)), ((), ())), preferred_element_type=jnp.float32
     )
-    pivot_sum = lax.psum(pivot_partial, PAR)
+    pivot_sum = pivot_partial
+    for mesh_axis in ("par_0", "par_1"):
+        pivot_sum = lax.psum(pivot_sum, mesh_axis)
     pivot_block = pivot_sum / samples + shift_value[0] * identity_matrix
     inverse_factor = invert_factor(pivot_block, identity_matrix)
     return lax.dot_general(

time: 806 us -> 853 us (1.058)
  waiting for transfers between devices: 318 us -> 364 us
    psum x1 -> x2, waiting for transfers between devices: 151 us -> 194 us  [on_device(): pivot_sum = lax.psum(pivot_sum, mesh_axis)]
  transfers between devices with their start and end apart: 7 -> 8, of which waited for: 6 -> 7; matrix products, arithmetic and copies ran while one was open for 50% -> 47% of each run, Pallas kernels for 0% -> 0%
where the time goes in v1:
time: 853 us; the launch traced here: 843 us
  waiting for transfers between devices  364 us (43%)
  other arithmetic  274 us (32%)
  matrix products  107 us (13%)
  local copies, waits for them, and re-layouts  60.1 us (7%)
  between operations  20.6 us (2%)
  starting transfers between devices  16.7 us (2%)
    psum x2, waiting for transfers between devices, on_device(): pivot_sum = lax.psum(pivot_sum, mesh_axis)  194 us
    another operation x30, other arithmetic, invert_factor(): factor = jnp.linalg.cholesky(block)  167 us
    all_to_all x1, waiting for transfers between devices, on_device(): lax.all_to_all(jacobian, PAR, split_axis=1, concat_axis=0, tiled=True)  87.4 us
    another operation x3, other arithmetic, invert_factor(): lax.linalg.triangular_solve(factor, identity_matrix, left_side=True, lowe...  84.5 us
    another operation x15, matrix products, invert_factor(): lax.linalg.triangular_solve(factor, identity_matrix, left_side=True, lowe...  50.3 us
    all_gather x1, waiting for transfers between devices, spread(): lax.all_gather(own, axis, axis=0, tiled=True)[:len(lines)]  37.8 us
    reduce_scatter x1, waiting for transfers between devices, spread(): own = lax.psum_scatter(padded, axis, scatter_dimension=0, tiled=True)  35.1 us
    another operation x14, matrix products, invert_factor(): factor = jnp.linalg.cholesky(block)  25.9 us
  transfers between devices with their start and end apart: 8, of which 7 were waited for; matrix products, arithmetic and copies ran while one was open for 47% of the time, Pallas kernels for 0%

profile of v1, /device:TPU:8, one launch (start us, length us, event | category | flops | bytes accessed | tf_op | source)
XLA Modules:
  0.0 843.3 jit_solution(17203489413983541085)
XLA Ops:
  7.8 11.3 %all-to-all-start = ((s32[32,1,32]{2,1,0:T(1,128)}), s32[32,1,32]{2,1,0:T(1,128)S(1)}, u32[]{:S(2)}, u32[]{:S(2)}) async-start(s32[32,1,32]{2,1,0:T(1,128)} %broadcast_in_dim.23), calls=%async_computation | async-start | bytes 32768 | tf_op jit(solution)/shard_map/all_to_all | solution.py:13
  40.2 87.4 %all-to-all-done.1 = bf16[32,32,2048]{2,0,1:T(8,128)(2,1)} async-done(((bf16[32,32,2048]{2,0,1:T(8,128)(2,1)}), bf16[32,32,2048]{2,0,1:T(8,128)(2,1)}, u32[]{:S(2)}, u32[]{:S(2)}) %all-to-all-start.1) | async-done | bytes 4194336 | tf_op jit(solution)/shard_map/all_to_all | solution.py:56
  127.6 11.6 %gather_fusion = bf16[1024,2048]{1,0:T(8,128)(2,1)} fusion(bf16[1024,2048]{1,0:T(8,128)(2,1)} %bitcast.1, s32[1024]{0:T(1024)S(1)} %fusion.77), kind=kCustom, calls=%fused_computation | custom fusion | bytes 8392704 | tf_op jit(solution)/shard_map/jit(_take)/gather | solution.py:59
  143.2 35.1 %reduce-scatter.6.cloned.1.call-done = bf16[128,2048]{1,0:T(8,128)(2,1)} async-done(((bf16[1024,2048]{1,0:T(8,128)(2,1)}), bf16[128,2048]{1,0:T(8,128)(2,1)}) %reduce-scatter.6.cloned.1.call-update) | async-done | bytes 524304 | tf_op jit(solution)/shard_map/reduce_scatter | solution.py:39
  178.4 37.8 %all-gather.2.cloned.1.call-done = bf16[1024,2048]{1,0:T(8,128)(2,1)} async-done(((bf16[128,2048]{1,0:T(8,128)(2,1)}), bf16[1024,2048]{1,0:T(8,128)(2,1)}) %all-gather.2.cloned.1.call-update) | async-done | bytes 4194320 | tf_op jit(solution)/shard_map/all_gather | solution.py:40
  216.2 13.5 %fusion.85 = f32[1024,1024]{0,1:T(8,128)} fusion(s32[]{:T(128)S(6)} %select_n.64, bf16[1024,2048]{1,0:T(8,128)(2,1)} %all-gather.2.cloned.1.call-done), kind=kOutput, calls=%fused_computation.182 | convolution fusion | flops 4303355904 | bytes 8388612 | tf_op jit(solution)/shard_map/dot_general | solution.py:77
  229.8 110.0 %all-reduce.4.cloned.1.call-done = f32[1024,1024]{0,1:T(8,128)} async-done(((f32[1024,1024]{0,1:T(8,128)}), f32[1024,1024]{0,1:T(8,128)}) %all-reduce.4.cloned.1.call-update) | async-done | bytes 4194320 | tf_op jit(solution)/shard_map/psum | solution.py:82
  344.5 9.8 %fusion.11 = f32[1024,1024]{0,1:T(8,128)} fusion(bf16[1024,2048]{1,0:T(8,128)(2,1)S(1)} %copy-done.2, pred[1024]{0:T(1024)(128)(4,1)S(1)} %compare_and_fusion, s32[]{:T(128)S(6)} %select_n.64, bf16[1024,2048]{1,0:T(8,128)(2,1)} %all-gather.2.cloned.1.call-done), kind=kOutput, calls=%fused_computation.26 | convolution fusion | flops 4305453056 | bytes 12583940 | tf_op jit(solution)/shard_map/dot_general | solution.py:64
  354.4 84.2 %all-reduce.6.cloned.1.call-done = f32[1024,1024]{0,1:T(8,128)} async-done(((f32[1024,1024]{0,1:T(8,128)}), f32[1024,1024]{0,1:T(8,128)}) %all-reduce.6.cloned.1.call-update) | async-done | bytes 4194320 | tf_op jit(solution)/shard_map/psum | solution.py:82
  455.4 11.7 %cholesky.222 = f32[128,128]{1,0:T(8,128)S(1)} custom-call(f32[128,128]{1,0:T(8,128)S(1)} %cholesky.577), custom_call_target="Cholesky" | custom-call | tf_op jit(solution)/shard_map/jit(cholesky)/cholesky | solution.py:51
  467.3 9.8 %custom-call.62 = f32[1,128,128]{1,2,0:T(8,128)S(1)} custom-call(f32[1,128,128]{2,1,0:T(8,128)S(1)} %get-tuple-element.71), custom_call_target="InvertDiagBlocksLowerTriangular" | custom-call | tf_op jit(solution)/shard_map/jit(cholesky)/cholesky | solution.py:51
  480.4 11.7 %cholesky.243 = f32[128,128]{1,0:T(8,128)S(1)} custom-call(f32[128,128]{1,0:T(8,128)S(1)} %cholesky.581), custom_call_target="Cholesky" | custom-call | tf_op jit(solution)/shard_map/jit(cholesky)/cholesky | solution.py:51
  492.7 9.8 %custom-call.63 = f32[1,128,128]{1,2,0:T(8,128)S(1)} custom-call(f32[1,128,128]{2,1,0:T(8,128)S(1)} %get-tuple-element.69), custom_call_target="InvertDiagBlocksLowerTriangular" | custom-call | tf_op jit(solution)/shard_map/jit(cholesky)/cholesky | solution.py:51
  508.0 11.7 %cholesky.466 = f32[128,128]{1,0:T(8,128)S(1)} custom-call(f32[128,128]{1,0:T(8,128)S(1)} %cholesky.586), custom_call_target="Cholesky" | custom-call | tf_op jit(solution)/shard_map/jit(cholesky)/cholesky | solution.py:51
  520.5 9.8 %custom-call.64 = f32[1,128,128]{1,2,0:T(8,128)S(1)} custom-call(f32[1,128,128]{2,1,0:T(8,128)S(1)} %get-tuple-element.67), custom_call_target="InvertDiagBlocksLowerTriangular" | custom-call | tf_op jit(solution)/shard_map/jit(cholesky)/cholesky | solution.py:51
  534.8 11.7 %cholesky.485 = f32[128,128]{1,0:T(8,128)S(1)} custom-call(f32[128,128]{1,0:T(8,128)S(1)} %cholesky.591), custom_call_target="Cholesky" | custom-call | tf_op jit(solution)/shard_map/jit(cholesky)/cholesky | solution.py:51
  561.4 12.1 %cholesky.504 = f32[128,128]{1,0:T(8,128)S(1)} custom-call(f32[128,128]{1,0:T(8,128)S(1)} %cholesky.596), custom_call_target="Cholesky" | custom-call | tf_op jit(solution)/shard_map/jit(cholesky)/cholesky | solution.py:51
  574.3 9.8 %custom-call.66 = f32[1,128,128]{1,2,0:T(8,128)S(1)} custom-call(f32[1,128,128]{2,1,0:T(8,128)S(1)} %get-tuple-element.63), custom_call_target="InvertDiagBlocksLowerTriangular" | custom-call | tf_op jit(solution)/shard_map/jit(cholesky)/cholesky | solution.py:51
  588.4 11.7 %cholesky.524 = f32[128,128]{1,0:T(8,128)S(1)} custom-call(f32[128,128]{1,0:T(8,128)S(1)} %cholesky.601), custom_call_target="Cholesky" | custom-call | tf_op jit(solution)/shard_map/jit(cholesky)/cholesky | solution.py:51
  614.5 11.7 %cholesky.544 = f32[128,128]{1,0:T(8,128)S(1)} custom-call(f32[128,128]{1,0:T(8,128)S(1)} %cholesky.606), custom_call_target="Cholesky" | custom-call | tf_op jit(solution)/shard_map/jit(cholesky)/cholesky | solution.py:51
  627.0 9.8 %custom-call.68 = f32[1,128,128]{1,2,0:T(8,128)S(1)} custom-call(f32[1,128,128]{2,1,0:T(8,128)S(1)} %get-tuple-element.59), custom_call_target="InvertDiagBlocksLowerTriangular" | custom-call | tf_op jit(solution)/shard_map/jit(cholesky)/cholesky | solution.py:51
  639.8 11.7 %cholesky.562 = f32[128,128]{1,0:T(8,128)S(1)} custom-call(f32[128,128]{1,0:T(8,128)S(1)} %convolution_subtract_fusion.11), custom_call_target="Cholesky" | custom-call | tf_op jit(solution)/shard_map/jit(cholesky)/cholesky | solution.py:51
  666.8 24.0 %while.1 = (s32[]{:T(128)}, f32[1024,1024]{0,1:T(8,128)}, s32[8,2]{0,1:T(2,128)S(1)}, f32[8,128,128]{2,1,0:T(8,128)S(1)}, s32[]{:T(128)}) while((s32[]{:T(128)}, f32[1024,1024]{0,1:T(8,128)}, s32[8,2]{0,1:T(2,128)S(1)}, f32[8,128,128]{2,1,0:T(8,128)S(1)}, s32[]{:T(128)}) %tuple.51), condition=%wide.while_cond, body=%wide.while_body.sunk | while | flops 2 | bytes 393329 | solution.py:52
  690.7 79.6 %custom-call.69 = f32[8,128,128]{1,2,0:T(8,128)} custom-call(f32[8,128,128]{2,1,0:T(8,128)S(1)} %get-tuple-element.14), custom_call_target="InvertDiagBlocksLowerTriangular" | custom-call | tf_op jit(solution)/shard_map/triangular_solve | solution.py:52
  (159 shorter events, 198.9 us)
Async XLA Ops:
  7.8 21.0 %all-to-all-start = ((s32[32,1,32]{2,1,0:T(1,128)}), s32[32,1,32]{2,1,0:T(1,128)S(1)}, u32[]{:S(2)}, u32[]{:S(2)}) async-start(s32[32,1,32]{2,1,0:T(1,128)} %broadcast_in_dim.23), calls=%async_computation | async-start | bytes 32768 | tf_op jit(solution)/shard_map/all_to_all | solution.py:13
  28.8 98.8 %all-to-all-start.1 = ((bf16[32,32,2048]{2,0,1:T(8,128)(2,1)}), bf16[32,32,2048]{2,0,1:T(8,128)(2,1)}, u32[]{:S(2)}, u32[]{:S(2)}) async-start(bf16[32,32,2048]{2,0,1:T(8,128)(2,1)} %bitcast.117), calls=%async_computation.1 | async-start | bytes 8388608 | tf_op jit(solution)/shard_map/all_to_all | solution.py:56
  33.8 144.5 %reduce-scatter.6.cloned.1.call-start = ((), (), s32[]{:S(2)}) async-start(), calls=%async_computation.5 | async-start | bytes 4718592 | tf_op jit(solution)/shard_map/reduce_scatter | solution.py:39
  143.1 73.1 %all-gather.2.cloned.1.call-start = ((), (), s32[]{:S(2)}) async-start(), calls=%async_computation.6 | async-start | bytes 4718592 | tf_op jit(solution)/shard_map/all_gather | solution.py:40
  178.4 161.5 %all-reduce.4.cloned.1.call-start = ((), (), s32[]{:S(2)}) async-start(), calls=%async_computation.8 | async-start | bytes 8388608 | tf_op jit(solution)/shard_map/psum | solution.py:82
  229.7 208.9 %all-reduce.6.cloned.1.call-start = ((), (), s32[]{:S(2)}) async-start(), calls=%async_computation.9 | async-start | bytes 8388608 | tf_op jit(solution)/shard_map/psum | solution.py:82
  339.8 461.4 %reduce-scatter.8.cloned.1.call-start = ((), (), s32[]{:S(2)}) async-start(), calls=%async_computation.7 | async-start | bytes 4718592 | tf_op jit(solution)/shard_map/reduce_scatter | solution.py:46
  340.7 3.7 copy-start.2
  354.4 473.2 %reduce-scatter.10.cloned.1.call-start = ((), (), s32[]{:S(2)}) async-start(), calls=%async_computation.10 | async-start | bytes 655360
  453.5 2.0 copy-start.3
  503.6 2.0 copy-start
  770.3 7.4 copy-start.1
  772.9 7.6 copy-start.4
Sparse Core Ops, SparseCore 0:
  143.3 35.0 reduce-scatter.5
  180.2 35.9 all-gather.1
  229.9 109.9 all-reduce.3
  342.0 96.5 all-reduce.5
  441.0 55.2 reduce-scatter.7
  803.4 24.1 reduce-scatter.9
